TPU v7x, 256 devices: a whole 4x4x8 slice. The times are simulated.
256 devices in a mesh: samp: 8 (over z), arow: 4 (over y), acol: 8 (over x, core).
Axes of the slice: x: 4, y: 4, z: 8, core: 2. Of those that a mesh axis runs over, the one named last changes fastest.
Arguments:
- embeddings: bfloat16 [393216, 768], P(('samp', 'arow', 'acol')), may hold values from -6 to 6
- anchors: bfloat16 [65536, 768], P(('arow', 'acol')), may hold values from -6 to 6
- subspace: bfloat16 [65536, 64], P(('arow', 'acol')), may hold values from -3 to 3
- nearest: int32 [393216, 8], P(('samp', 'arow', 'acol')), may hold values from 0 to 65535, as said below
Outputs:
- gram_product: float32 [65536, 64], P(('arow', 'acol'))
Inputs may be any that keep to these rules, and one draw needn't show every extreme that they name: `nearest`: anchor shard o holds anchors 2048 * o to 2048 * (o + 1) - 1. The rows of one device name anchors of every one of the 32 shards, and within each of them only anchors of one aligned block of 128. The 8 anchors of a row are distinct.
All inputs are finite; a program needn't handle non-finite values.
Results may differ from a plain program's by a relative error of at most 0.0003.
Values may be sent and summed in bfloat16 or wider, within the bound.
A program may use at most 128 MiB of HBM per device.

v0:
```python
import jax
import jax.numpy as jnp
from jax import lax
from jax.sharding import PartitionSpec as P

D = 768
COLS = 64
CAND = 8
BA = 128


def from_everyone(value, axis):
    devices = lax.axis_size(axis)
    return lax.all_to_all(
        jnp.broadcast_to(value[None], (devices, *value.shape)), axis, 0, 0, tiled=True
    )


def in_order(tiles, dim):
    shape = list(tiles.shape[1:])
    shape[dim] *= tiles.shape[0]
    return jnp.moveaxis(tiles, 0, dim).reshape(shape)


def gather_directly(value, axis, dim):
    tiles = from_everyone(value, axis)
    return in_order(tiles, dim)


def sent_together(arrays, axis, split_dim, concat_dim, along):
    both = jnp.concatenate(arrays, axis=along)
    result, at, outs = (
        lax.all_to_all(both, axis, split_axis=split_dim, concat_axis=concat_dim, tiled=True),
        0,
        [],
    )
    for a in arrays:
        outs.append(lax.slice_in_dim(result, at, at + a.shape[along], axis=along))
        at += a.shape[along]
    return tuple(outs)


def total_of_pieces(value, axis):
    return lax.all_gather(value, axis).sum(0)


def per_device(embeddings, anchors, subspace, nearest):
    grid_rows = lax.axis_size("arow")
    grid_cols = lax.axis_size("acol")
    owners = grid_rows * grid_cols
    self_index = lax.axis_index("arow") * grid_cols + lax.axis_index("acol")
    shard_size = anchors.shape[0]
    shard_blocks = shard_size // BA
    owner_of = nearest // shard_size
    block_of = nearest % shard_size // BA
    slot_of = owner_of * BA + nearest % BA
    matches = owner_of.reshape(-1)[:, None] == jnp.arange(owners, dtype=jnp.int32)[None, :]
    wanted = jnp.max(jnp.where(matches, block_of.reshape(-1)[:, None], -1), axis=0)
    table = gather_directly(wanted[None, :], ("arow", "acol"), 0)
    asked = lax.dynamic_index_in_dim(table, self_index, axis=1, keepdims=False)
    anchor_out = anchors.reshape(shard_blocks, BA, D)[asked]
    panel_out = subspace.reshape(shard_blocks, BA, COLS)[asked]
    anchor_in, panel_in = sent_together((anchor_out, panel_out), ("arow", "acol"), 0, 0, 2)
    total_slots = owners * BA
    flat_anchor = anchor_in.reshape(total_slots, D)
    flat_panel = panel_in.reshape(total_slots, COLS).astype(jnp.float32)
    anchor_scale = lax.rsqrt(jnp.mean(jnp.square(flat_anchor.astype(jnp.float32)), axis=1) + 1e-06)
    slot_iota = jnp.arange(total_slots, dtype=jnp.int32)
    row_total = embeddings.shape[0]
    block_rows = min(256, row_total)
    block_count = row_total // block_rows

    def one_block(outgoing, inputs):
        group_rows, group_slots = inputs
        rows_float = group_rows.astype(jnp.float32)
        row_scale = lax.rsqrt(jnp.mean(rows_float * rows_float, axis=1) + 1e-06)
        dense = lax.dot_general(
            group_rows, flat_anchor, (((1,), (1,)), ((), ())), preferred_element_type=jnp.float32
        )
        equal_list = [group_slots[:, k : k + 1] == slot_iota[None, :] for k in range(CAND)]
        dots = jnp.stack(
            [jnp.sum(jnp.where(equal, dense, 0.0), axis=1) for equal in equal_list], axis=1
        )
        scales = jnp.stack(
            [jnp.sum(jnp.where(equal, anchor_scale[None, :], 0.0), axis=1) for equal in equal_list],
            axis=1,
        )
        cosine = dots * row_scale[:, None] * scales / D
        kernel = jnp.exp((cosine - 1.0) / 0.05)
        weights = kernel / jnp.sum(kernel, axis=1, keepdims=True)
        zmatrix = jnp.zeros((group_rows.shape[0], total_slots), jnp.float32)
        for k in range(CAND):
            zmatrix = zmatrix + jnp.where(equal_list[k], weights[:, k : k + 1], 0.0)
        projected = jnp.dot(
            zmatrix, flat_panel, precision=lax.Precision.HIGHEST, preferred_element_type=jnp.float32
        )
        update = lax.dot_general(
            zmatrix,
            projected,
            (((0,), (0,)), ((), ())),
            precision=lax.Precision.HIGHEST,
            preferred_element_type=jnp.float32,
        )
        return (outgoing + update, None)

    outgoing, _ = lax.scan(
        one_block,
        jnp.zeros((total_slots, COLS), jnp.float32),
        (
            embeddings.reshape(block_count, block_rows, D),
            slot_of.reshape(block_count, block_rows, CAND),
        ),
    )
    returned = lax.all_to_all(
        outgoing.reshape(owners, BA, COLS),
        ("arow", "acol"),
        split_axis=0,
        concat_axis=0,
        tiled=True,
    )
    selector = (asked[None, :] == jnp.arange(shard_blocks, dtype=jnp.int32)[:, None]).astype(
        jnp.float32
    )
    mine = jnp.dot(
        selector,
        returned.reshape(owners, BA * COLS),
        precision=lax.Precision.HIGHEST,
        preferred_element_type=jnp.float32,
    )
    return total_of_pieces(mine.reshape(shard_size, COLS), "samp")


def solution(mesh):
    in_specs = (
        P(("samp", "arow", "acol"), None),
        P(("arow", "acol"), None),
        P(("arow", "acol"), None),
        P(("samp", "arow", "acol"), None),
    )
    out_specs = P(("arow", "acol"), None)
    return jax.shard_map(
        per_device, mesh=mesh, in_specs=in_specs, out_specs=out_specs, check_vma=False
    )
```

profile of v0, /device:TPU:32, one launch (start us, length us, event | category | flops | bytes accessed | tf_op | source)
XLA Modules:
  0.0 466.5 jit_solution(4500766932041155293)
XLA Ops:
  13.7 7.3 %all-to-all-start = ((s32[32,1,32]{2,1,0:T(1,128)}), s32[32,1,32]{2,1,0:T(1,128)S(1)}, u32[]{:S(2)}, u32[]{:S(2)}) async-start(s32[32,1,32]{2,1,0:T(1,128)} %broadcast_in_dim.219), calls=%async_computation | async-start | bytes 32768 | tf_op jit(solution)/shard_map/all_to_all | solution.py:14
  22.0 6.3 %all-to-all-done = s32[32,1,32]{2,1,0:T(1,128)S(1)} async-done(((s32[32,1,32]{2,1,0:T(1,128)}), s32[32,1,32]{2,1,0:T(1,128)S(1)}, u32[]{:S(2)}, u32[]{:S(2)}) %all-to-all-start) | async-done | bytes 4128 | tf_op jit(solution)/shard_map/all_to_all | solution.py:14
  33.4 3.6 gather_fusion
  37.1 7.2 %pad_maximum_fusion = bf16[32,128,832]{2,1,0:T(8,128)(2,1)} fusion(bf16[32,128,64]{2,1,0:T(8,128)(2,1)} %copy.37, bf16[32,128,768]{2,1,0:T(8,128)(2,1)} %gather_fusion), kind=kLoop, calls=%fused_computation.73 | loop fusion | flops 13631488 | bytes 13631488 | tf_op jit(solution)/shard_map/concatenate | solution.py:31
  44.3 10.5 %copy.38 = bf16[32,128,832]{1,2,0:T(8,128)(2,1)} copy(bf16[32,128,832]{2,1,0:T(8,128)(2,1)} %pad_maximum_fusion) | data formatting | bytes 13631488 | tf_op jit(solution)/shard_map/concatenate | solution.py:31
  54.7 4.9 %all-to-all-start.1 = ((bf16[32,128,832]{1,2,0:T(8,128)(2,1)}), bf16[32,128,832]{1,2,0:T(8,128)(2,1)}, u32[]{:S(2)}, u32[]{:S(2)}) async-start(bf16[32,128,832]{1,2,0:T(8,128)(2,1)} %copy.38), calls=%async_computation.1 | async-start | bytes 13631488 | tf_op jit(solution)/shard_map/all_to_all | solution.py:33
  59.7 84.3 %all-to-all-done.1 = bf16[32,128,832]{1,2,0:T(8,128)(2,1)} async-done(((bf16[32,128,832]{1,2,0:T(8,128)(2,1)}), bf16[32,128,832]{1,2,0:T(8,128)(2,1)}, u32[]{:S(2)}, u32[]{:S(2)}) %all-to-all-start.1) | async-done | bytes 6815776 | tf_op jit(solution)/shard_map/all_to_all | solution.py:33
  144.0 6.1 %slice.156 = bf16[32,128,768]{1,2,0:T(8,128)(2,1)} slice(bf16[32,128,832]{1,2,0:T(8,128)(2,1)} %all-to-all-done.1), slice={[0:32], [0:128], [0:768]} | slice | bytes 12582912 | tf_op jit(solution)/shard_map/slice | solution.py:38
  150.1 8.6 %copy.50 = bf16[32,128,768]{2,1,0:T(8,128)(2,1)} copy(bf16[32,128,768]{1,2,0:T(8,128)(2,1)} %slice.156) | data formatting | bytes 12582912
  158.7 4.1 multiply_reduce_fusion.1
  164.6 208.5 %while.14 = (s32[]{:T(128)}, f32[4096,64]{0,1:T(8,128)}, s32[6,256,8]{1,2,0:T(8,128)S(1)}, bf16[6,256,768]{2,1,0:T(8,128)(2,1)}, bf16[4096,768]{1,0:T(8,128)(2,1...) while((s32[]{:T(128)}, f32[4096,64]{0,1:T(8,128)}, ...), condition=%wide.region_21.22_spmd.clone.clone, body=%wide.region_2.21_spmd.clone.clone.sunk | while | flops 3312537600 | bytes 27335856 | solution.py:106
  166.0 14.2 %fusion.97 = (f32[256]{0:T(256)S(1)}, f32[256]{0:T(256)S(1)}, f32[256]{0:T(256)S(1)}, f32[256]{0:T(256)S(1)}, f32[256]{0:T(256)S(1)}, /*index=5*/f32[256]{0:T(25...) fusion(f32[4096]{0:T(1024)S(1)} %get-tuple-element.381, ...), kind=kOutput, calls=%fused_computation.37.clone.1 | convolution fusion | flops 1652551680 | bytes 6725636 | tf_op jit(solution)/shard_map/while/body/eval_jaxpr/dot_general | solution.py:77
  180.3 7.3 %fusion.100 = f32[256,4096]{1,0:T(8,128)S(1)} fusion(f32[256]{0:T(256)S(1)} %bitcast.176, f32[256]{0:T(256)S(1)} %bitcast.178, f32[256]{0:T(256)S(1)} %bitcast.180, f32[256]{0:T(256)S(1)} %bitcast.182, f32[256]{0:T(256)S(1)} %bitcast.184, f32[256]{0:T(256)S(1)} %bitcast.186, f32[256]{0:T(256)S(1)} %bitcast.188, f32[256]{0:T(256)S(1)} %bitcast.174, ...), kind=kLoop, calls=%fused_computation.38.clone.1.clone.1.clone.1 | loop fusion | flops 24117248 | bytes 4210688 | tf_op jit(solution)/shard_map/while/body/eval_jaxpr/dot_general | solution.py:94
  191.3 7.2 %convolution_add_fusion.2 = f32[4096,64]{0,1:T(8,128)S(1)} fusion(f32[256,64]{0,1:T(8,128)S(1)} %fusion.101, f32[256]{0:T(256)S(1)} %bitcast.177, f32[256]{0:T(256)S(1)} %bitcast.179, f32[256]{0:T(256)S(1)} %bitcast.181, f32[256]{0:T(256)S(1)} %bitcast.183, f32[256]{0:T(256)S(1)} %bitcast.185, f32[256]{0:T(256)S(1)} %bitcast.187, ...), kind=kOutput, calls=%fused_computation.35.clone.1 | convolution fusion | flops 829947904 | bytes 2179073 | tf_op jit(solution)/shard_map/while/body/eval_jaxpr/dot_general | solution.py:97
  200.7 14.2 %fusion.97 = (f32[256]{0:T(256)S(1)}, f32[256]{0:T(256)S(1)}, f32[256]{0:T(256)S(1)}, f32[256]{0:T(256)S(1)}, f32[256]{0:T(256)S(1)}, /*index=5*/f32[256]{0:T(25...) fusion(f32[4096]{0:T(1024)S(1)} %get-tuple-element.381, ...), kind=kOutput, calls=%fused_computation.37.clone.1 | convolution fusion | flops 1652551680 | bytes 6725636 | tf_op jit(solution)/shard_map/while/body/eval_jaxpr/dot_general | solution.py:77
  215.0 7.3 %fusion.100 = f32[256,4096]{1,0:T(8,128)S(1)} fusion(f32[256]{0:T(256)S(1)} %bitcast.176, f32[256]{0:T(256)S(1)} %bitcast.178, f32[256]{0:T(256)S(1)} %bitcast.180, f32[256]{0:T(256)S(1)} %bitcast.182, f32[256]{0:T(256)S(1)} %bitcast.184, f32[256]{0:T(256)S(1)} %bitcast.186, f32[256]{0:T(256)S(1)} %bitcast.188, f32[256]{0:T(256)S(1)} %bitcast.174, ...), kind=kLoop, calls=%fused_computation.38.clone.1.clone.1.clone.1 | loop fusion | flops 24117248 | bytes 4210688 | tf_op jit(solution)/shard_map/while/body/eval_jaxpr/dot_general | solution.py:94
  226.0 7.2 %convolution_add_fusion.2 = f32[4096,64]{0,1:T(8,128)S(1)} fusion(f32[256,64]{0,1:T(8,128)S(1)} %fusion.101, f32[256]{0:T(256)S(1)} %bitcast.177, f32[256]{0:T(256)S(1)} %bitcast.179, f32[256]{0:T(256)S(1)} %bitcast.181, f32[256]{0:T(256)S(1)} %bitcast.183, f32[256]{0:T(256)S(1)} %bitcast.185, f32[256]{0:T(256)S(1)} %bitcast.187, ...), kind=kOutput, calls=%fused_computation.35.clone.1 | convolution fusion | flops 829947904 | bytes 2179073 | tf_op jit(solution)/shard_map/while/body/eval_jaxpr/dot_general | solution.py:97
  235.4 14.2 %fusion.97 = (f32[256]{0:T(256)S(1)}, f32[256]{0:T(256)S(1)}, f32[256]{0:T(256)S(1)}, f32[256]{0:T(256)S(1)}, f32[256]{0:T(256)S(1)}, /*index=5*/f32[256]{0:T(25...) fusion(f32[4096]{0:T(1024)S(1)} %get-tuple-element.381, ...), kind=kOutput, calls=%fused_computation.37.clone.1 | convolution fusion | flops 1652551680 | bytes 6725636 | tf_op jit(solution)/shard_map/while/body/eval_jaxpr/dot_general | solution.py:77
  249.8 7.3 %fusion.100 = f32[256,4096]{1,0:T(8,128)S(1)} fusion(f32[256]{0:T(256)S(1)} %bitcast.176, f32[256]{0:T(256)S(1)} %bitcast.178, f32[256]{0:T(256)S(1)} %bitcast.180, f32[256]{0:T(256)S(1)} %bitcast.182, f32[256]{0:T(256)S(1)} %bitcast.184, f32[256]{0:T(256)S(1)} %bitcast.186, f32[256]{0:T(256)S(1)} %bitcast.188, f32[256]{0:T(256)S(1)} %bitcast.174, ...), kind=kLoop, calls=%fused_computation.38.clone.1.clone.1.clone.1 | loop fusion | flops 24117248 | bytes 4210688 | tf_op jit(solution)/shard_map/while/body/eval_jaxpr/dot_general | solution.py:94
  257.1 3.6 fusion.101
  260.7 7.2 %convolution_add_fusion.2 = f32[4096,64]{0,1:T(8,128)S(1)} fusion(f32[256,64]{0,1:T(8,128)S(1)} %fusion.101, f32[256]{0:T(256)S(1)} %bitcast.177, f32[256]{0:T(256)S(1)} %bitcast.179, f32[256]{0:T(256)S(1)} %bitcast.181, f32[256]{0:T(256)S(1)} %bitcast.183, f32[256]{0:T(256)S(1)} %bitcast.185, f32[256]{0:T(256)S(1)} %bitcast.187, ...), kind=kOutput, calls=%fused_computation.35.clone.1 | convolution fusion | flops 829947904 | bytes 2179073 | tf_op jit(solution)/shard_map/while/body/eval_jaxpr/dot_general | solution.py:97
  270.1 14.2 %fusion.97 = (f32[256]{0:T(256)S(1)}, f32[256]{0:T(256)S(1)}, f32[256]{0:T(256)S(1)}, f32[256]{0:T(256)S(1)}, f32[256]{0:T(256)S(1)}, /*index=5*/f32[256]{0:T(25...) fusion(f32[4096]{0:T(1024)S(1)} %get-tuple-element.381, ...), kind=kOutput, calls=%fused_computation.37.clone.1 | convolution fusion | flops 1652551680 | bytes 6725636 | tf_op jit(solution)/shard_map/while/body/eval_jaxpr/dot_general | solution.py:77
  284.5 7.3 %fusion.100 = f32[256,4096]{1,0:T(8,128)S(1)} fusion(f32[256]{0:T(256)S(1)} %bitcast.176, f32[256]{0:T(256)S(1)} %bitcast.178, f32[256]{0:T(256)S(1)} %bitcast.180, f32[256]{0:T(256)S(1)} %bitcast.182, f32[256]{0:T(256)S(1)} %bitcast.184, f32[256]{0:T(256)S(1)} %bitcast.186, f32[256]{0:T(256)S(1)} %bitcast.188, f32[256]{0:T(256)S(1)} %bitcast.174, ...), kind=kLoop, calls=%fused_computation.38.clone.1.clone.1.clone.1 | loop fusion | flops 24117248 | bytes 4210688 | tf_op jit(solution)/shard_map/while/body/eval_jaxpr/dot_general | solution.py:94
  295.4 7.2 %convolution_add_fusion.2 = f32[4096,64]{0,1:T(8,128)S(1)} fusion(f32[256,64]{0,1:T(8,128)S(1)} %fusion.101, f32[256]{0:T(256)S(1)} %bitcast.177, f32[256]{0:T(256)S(1)} %bitcast.179, f32[256]{0:T(256)S(1)} %bitcast.181, f32[256]{0:T(256)S(1)} %bitcast.183, f32[256]{0:T(256)S(1)} %bitcast.185, f32[256]{0:T(256)S(1)} %bitcast.187, ...), kind=kOutput, calls=%fused_computation.35.clone.1 | convolution fusion | flops 829947904 | bytes 2179073 | tf_op jit(solution)/shard_map/while/body/eval_jaxpr/dot_general | solution.py:97
  304.8 14.2 %fusion.97 = (f32[256]{0:T(256)S(1)}, f32[256]{0:T(256)S(1)}, f32[256]{0:T(256)S(1)}, f32[256]{0:T(256)S(1)}, f32[256]{0:T(256)S(1)}, /*index=5*/f32[256]{0:T(25...) fusion(f32[4096]{0:T(1024)S(1)} %get-tuple-element.381, ...), kind=kOutput, calls=%fused_computation.37.clone.1 | convolution fusion | flops 1652551680 | bytes 6725636 | tf_op jit(solution)/shard_map/while/body/eval_jaxpr/dot_general | solution.py:77
  319.2 7.3 %fusion.100 = f32[256,4096]{1,0:T(8,128)S(1)} fusion(f32[256]{0:T(256)S(1)} %bitcast.176, f32[256]{0:T(256)S(1)} %bitcast.178, f32[256]{0:T(256)S(1)} %bitcast.180, f32[256]{0:T(256)S(1)} %bitcast.182, f32[256]{0:T(256)S(1)} %bitcast.184, f32[256]{0:T(256)S(1)} %bitcast.186, f32[256]{0:T(256)S(1)} %bitcast.188, f32[256]{0:T(256)S(1)} %bitcast.174, ...), kind=kLoop, calls=%fused_computation.38.clone.1.clone.1.clone.1 | loop fusion | flops 24117248 | bytes 4210688 | tf_op jit(solution)/shard_map/while/body/eval_jaxpr/dot_general | solution.py:94
  330.1 7.2 %convolution_add_fusion.2 = f32[4096,64]{0,1:T(8,128)S(1)} fusion(f32[256,64]{0,1:T(8,128)S(1)} %fusion.101, f32[256]{0:T(256)S(1)} %bitcast.177, f32[256]{0:T(256)S(1)} %bitcast.179, f32[256]{0:T(256)S(1)} %bitcast.181, f32[256]{0:T(256)S(1)} %bitcast.183, f32[256]{0:T(256)S(1)} %bitcast.185, f32[256]{0:T(256)S(1)} %bitcast.187, ...), kind=kOutput, calls=%fused_computation.35.clone.1 | convolution fusion | flops 829947904 | bytes 2179073 | tf_op jit(solution)/shard_map/while/body/eval_jaxpr/dot_general | solution.py:97
  339.6 14.2 %fusion.97 = (f32[256]{0:T(256)S(1)}, f32[256]{0:T(256)S(1)}, f32[256]{0:T(256)S(1)}, f32[256]{0:T(256)S(1)}, f32[256]{0:T(256)S(1)}, /*index=5*/f32[256]{0:T(25...) fusion(f32[4096]{0:T(1024)S(1)} %get-tuple-element.381, ...), kind=kOutput, calls=%fused_computation.37.clone.1 | convolution fusion | flops 1652551680 | bytes 6725636 | tf_op jit(solution)/shard_map/while/body/eval_jaxpr/dot_general | solution.py:77
  353.9 7.3 %fusion.100 = f32[256,4096]{1,0:T(8,128)S(1)} fusion(f32[256]{0:T(256)S(1)} %bitcast.176, f32[256]{0:T(256)S(1)} %bitcast.178, f32[256]{0:T(256)S(1)} %bitcast.180, f32[256]{0:T(256)S(1)} %bitcast.182, f32[256]{0:T(256)S(1)} %bitcast.184, f32[256]{0:T(256)S(1)} %bitcast.186, f32[256]{0:T(256)S(1)} %bitcast.188, f32[256]{0:T(256)S(1)} %bitcast.174, ...), kind=kLoop, calls=%fused_computation.38.clone.1.clone.1.clone.1 | loop fusion | flops 24117248 | bytes 4210688 | tf_op jit(solution)/shard_map/while/body/eval_jaxpr/dot_general | solution.py:94
  364.8 7.2 %convolution_add_fusion.2 = f32[4096,64]{0,1:T(8,128)S(1)} fusion(f32[256,64]{0,1:T(8,128)S(1)} %fusion.101, f32[256]{0:T(256)S(1)} %bitcast.177, f32[256]{0:T(256)S(1)} %bitcast.179, f32[256]{0:T(256)S(1)} %bitcast.181, f32[256]{0:T(256)S(1)} %bitcast.183, f32[256]{0:T(256)S(1)} %bitcast.185, f32[256]{0:T(256)S(1)} %bitcast.187, ...), kind=kOutput, calls=%fused_computation.35.clone.1 | convolution fusion | flops 829947904 | bytes 2179073 | tf_op jit(solution)/shard_map/while/body/eval_jaxpr/dot_general | solution.py:97
  374.4 20.2 %all_to_all.15 = f32[32,128,64]{1,2,0:T(8,128)S(1)} all-to-all(f32[32,128,64]{1,2,0:T(8,128)S(1)} %copy_bitcast_fusion), channel_id=1, replica_groups=mesh['samp'=8,'arow'=4,'acol'=8] {'arow','acol'}, dimensions={0} | all-to-all | bytes 2097152 | tf_op jit(solution)/shard_map/all_to_all | solution.py:114
  404.4 52.0 %all-gather.2.cloned.1.call-done = f32[8,2048,64]{1,2,0:T(8,128)} async-done(((f32[1,2048,64]{1,2,0:T(8,128)}), f32[8,2048,64]{1,2,0:T(8,128)}) %all-gather.2.cloned.1.call-update) | async-done | bytes 4194320 | tf_op jit(solution)/shard_map/all_gather | solution.py:44
  (117 shorter events, 61.0 us)
Async XLA Ops:
  6.5 26.9 %copy-start = (bf16[2048,768]{1,0:T(8,128)(2,1)S(1)}, bf16[2048,768]{1,0:T(8,128)(2,1)}, u32[]{:S(2)}) copy-start(bf16[2048,768]{1,0:T(8,128)(2,1)} %param.7) | copy-start | bytes 9437188
  13.7 14.6 %all-to-all-start = ((s32[32,1,32]{2,1,0:T(1,128)}), s32[32,1,32]{2,1,0:T(1,128)S(1)}, u32[]{:S(2)}, u32[]{:S(2)}) async-start(s32[32,1,32]{2,1,0:T(1,128)} %broadcast_in_dim.219), calls=%async_computation | async-start | bytes 32768 | tf_op jit(solution)/shard_map/all_to_all | solution.py:14
  29.1 0.6 copy-start.4
  54.7 89.3 %all-to-all-start.1 = ((bf16[32,128,832]{1,2,0:T(8,128)(2,1)}), bf16[32,128,832]{1,2,0:T(8,128)(2,1)}, u32[]{:S(2)}, u32[]{:S(2)}) async-start(bf16[32,128,832]{1,2,0:T(8,128)(2,1)} %copy.38), calls=%async_computation.1 | async-start | bytes 13631488 | tf_op jit(solution)/shard_map/all_to_all | solution.py:33
  59.6 396.8 %all-gather.2.cloned.1.call-start = ((), (), s32[]{:S(2)}) async-start(), calls=%async_computation.3 | async-start | bytes 4718592 | tf_op jit(solution)/shard_map/all_gather | solution.py:44
  187.7 3.6 copy-start.2
  198.5 1.0 copy-start.3
  222.4 3.6 copy-start.2
  233.2 1.0 copy-start.3
  257.1 3.6 copy-start.2
  267.9 1.0 copy-start.3
  291.8 3.6 copy-start.2
  302.6 1.0 copy-start.3
  326.5 3.6 copy-start.2
  337.4 1.0 copy-start.3
  361.2 3.6 copy-start.2
  372.1 1.0 copy-start.3
  374.4 22.5 %copy-start.5 = (s32[32]{0:T(128)S(1)}, s32[32]{0:T(128)}, u32[]{:S(2)}) copy-start(s32[32]{0:T(128)} %copy-done.4) | copy-start | bytes 388
  396.9 62.8 %copy-start.1 = (bf16[2048,768]{1,0:T(8,128)(2,1)S(1)}, bf16[2048,768]{1,0:T(8,128)(2,1)}, u32[]{:S(2)}) copy-start(bf16[2048,768]{1,0:T(8,128)(2,1)} %param.7) | copy-start | bytes 9437188
Sparse Core Ops, SparseCore 0:
  404.5 51.8 all-gather.1
where the time goes:
time: 471 us; the launch traced here: 467 us
  matrix products  153 us (32%)
  waiting for transfers between devices  143 us (30%)
  other arithmetic  68.2 us (14%)
  local copies, waits for them, and re-layouts  56.2 us (12%)
  blocking collectives  20.2 us (4%)
  between operations  13.5 us (3%)
  starting transfers between devices  12.3 us (3%)
    dot_general x6, matrix products, one_block(): lax.dot_general(group_rows, flat_anchor, (((1,), (1,)), ((), ())), prefer...  85.2 us
    all_to_all x1, waiting for transfers between devices, sent_together(): lax.all_to_all(both, axis, split_axis=split_dim, concat_axis=concat_dim,...  84.3 us
    all_gather x1, waiting for transfers between devices, total_of_pieces(): return lax.all_gather(value, axis).sum(0)  52 us
    dot_general x6, other arithmetic, one_block(): jnp.dot(zmatrix, flat_panel, precision=lax.Precision.HIGHEST, preferred_e...  43.9 us
    dot_general x6, matrix products, one_block(): lax.dot_general(zmatrix, projected, (((0,), (0,)), ((), ())), precision=l...  43.5 us
    dot_general x6, matrix products, one_block(): jnp.dot(zmatrix, flat_panel, precision=lax.Precision.HIGHEST, preferred_e...  21.4 us
    all_to_all x1, blocking collectives, per_device(): lax.all_to_all(outgoing.reshape(owners, BA, COLS), ('arow', 'acol'), spli...  20.2 us
    concatenate x1, local copies, waits for them, and re-layouts, sent_together(): both = jnp.concatenate(arrays, axis=along)  10.5 us
  transfers between devices with their start and end apart: 3, of which 3 were waited for; matrix products, arithmetic and copies ran while one was open for 0% of the time, Pallas kernels for 0%

commit v1 on v0

v1 whole, which is shorter than its diff:
```python
import functools

import jax
import jax.numpy as jnp
from jax import lax
from jax.experimental import pallas as pl
from jax.experimental.pallas import tpu as pltpu
from jax.sharding import PartitionSpec as P

D = 768
COLS = 64
CAND = 8
BA = 128
OWNERS = 32
BLOCKS = 16
ROWS = 1536
PLANES = 8
RC = 256
MESH = pl.DeviceIdType.MESH
SCALE = 20.0 * 1.4426950408889634 / D

ORDER = (
    (0, 0), (0, 1), (1, 0), (0, 3), (3, 0), (0, 2), (2, 0), (1, 1),
    (3, 3), (1, 3), (3, 1), (2, 2), (2, 1), (1, 2), (2, 3), (3, 2),
)


def packed(which):
    word = sum(offset[which] << (2 * t) for t, offset in enumerate(ORDER))
    return word - (1 << 32) if word >= 1 << 31 else word


KY, KX = packed(0), packed(1)


def digit(word, t):
    return lax.shift_right_logical(jnp.int32(word), jnp.int32(2) * t) & 3


def nt(a, b):
    return lax.dot_general(a, b, (((1,), (1,)), ((), ())), preferred_element_type=jnp.float32)


def nn(a, b):
    return lax.dot_general(a, b, (((1,), (0,)), ((), ())), preferred_element_type=jnp.float32)


def kernel(
    emb_hbm, anc_hbm, sub_ref, near_ref, out_ref,
    emb, anc, sub, best, ask, table, table_s, bits_s,
    stage_a, stage_v, slots, panel, panel1, words, rscale, high, low, sums, lhs,
    give, back, acc, part, whole,
    local_sem, table_sem, ask_s, ask_r, anc_s, anc_r, pan_s, pan_r, ret_s, ret_r,
    red_s, red_r, gat_s, gat_r,
):
    z = lax.axis_index("samp")
    y = lax.axis_index("arow")
    a = lax.axis_index("acol")
    x = lax.div(a, 2)
    c = lax.rem(a, 2)
    me = y * 8 + a

    def receiver(t, dc):
        sign = 1 - 2 * c
        py = lax.rem(y + 4 + sign * digit(KY, t), 4)
        px = lax.rem(x + 4 + sign * digit(KX, t), 4)
        return (z, py, px * 2 + lax.rem(c + dc, 2))

    def holder(t, dc):
        core = lax.rem(c + dc, 2)
        sign = 1 - 2 * core
        py = lax.rem(y + 4 - sign * digit(KY, t), 4)
        px = lax.rem(x + 4 - sign * digit(KX, t), 4)
        return (z, py, px * 2 + core)

    emb_copy = pltpu.make_async_copy(emb_hbm, emb, local_sem.at[0])
    anc_copy = pltpu.make_async_copy(anc_hbm, anc, local_sem.at[1])
    anc_copy.start()
    emb_copy.start()

    barrier = pltpu.get_barrier_semaphore()

    @pl.loop(1, OWNERS)
    def _(i):
        p = lax.rem(me + i, OWNERS)
        pl.semaphore_signal(
            barrier, inc=1, device_id=(z, lax.div(p, 8), lax.rem(p, 8)), device_id_type=MESH
        )

    @pl.loop(1, PLANES)
    def _(i):
        pl.semaphore_signal(
            barrier, inc=1, device_id=(lax.rem(z + i, PLANES), y, a), device_id_type=MESH
        )

    near = near_ref[...]
    owner = near >> 11
    block = (near >> 7) & 15
    for o in range(OWNERS):
        m = jnp.where(owner == o, block, 0)
        parts = [m[:, i * 128 : (i + 1) * 128] for i in range(ROWS // 128)]
        while len(parts) > 1:
            parts = [
                jnp.maximum(parts[i], parts[i + 1]) if i + 1 < len(parts) else parts[i]
                for i in range(0, len(parts), 2)
            ]
        best[o : o + 1, :] = jnp.max(parts[0], axis=0, keepdims=True)
    wanted = jnp.broadcast_to(jnp.max(best[...], axis=1, keepdims=True), (OWNERS, 128))
    for o in range(OWNERS):
        ask[o] = wanted[o : o + 1, :]

    pl.semaphore_wait(barrier, OWNERS - 1 + PLANES - 1)

    def ask_copy(t, dc):
        n = 2 * t + dc
        to = holder(t, dc)
        return pltpu.make_async_remote_copy(
            src_ref=ask.at[to[1] * 8 + to[2]], dst_ref=table.at[n],
            send_sem=ask_s.at[n], recv_sem=ask_r.at[n], device_id=to, device_id_type=MESH,
        )

    def anchor_copy(t, dc):
        n = 2 * t + dc
        return pltpu.make_async_remote_copy(
            src_ref=stage_a.at[n], dst_ref=slots.at[t, pl.ds(dc * BA, BA)],
            send_sem=anc_s.at[n], recv_sem=anc_r.at[n],
            device_id=receiver(t, dc), device_id_type=MESH,
        )

    def panel_copy(t, dc):
        n = 2 * t + dc
        return pltpu.make_async_remote_copy(
            src_ref=stage_v.at[n], dst_ref=panel.at[n],
            send_sem=pan_s.at[n], recv_sem=pan_r.at[n],
            device_id=receiver(t, dc), device_id_type=MESH,
        )

    def return_copy(t, dc):
        n = 2 * t + dc
        return pltpu.make_async_remote_copy(
            src_ref=give.at[n], dst_ref=back.at[n],
            send_sem=ret_s.at[n], recv_sem=ret_r.at[n],
            device_id=holder(t, dc), device_id_type=MESH,
        )

    def each(body):
        body(jnp.int32(0), 1)

        @pl.loop(1, 16)
        def _(t):
            body(t, 0)
            body(t, 1)

    each(lambda t, dc: ask_copy(t, dc).start())

    for b in range(BLOCKS):
        sub[b] = sub_ref[:, b * BA : (b + 1) * BA]
    panel1[COLS:, :] = jnp.ones((BA - COLS, 2 * BA), jnp.bfloat16)
    table[0] = ask[me]

    @pl.loop(0, 16)
    def _(t):
        for dc in range(2):
            h = holder(t, dc)
            bits_s[2 * t + dc] = lax.shift_left(jnp.int32(1), h[1] * 8 + h[2])

    anc_copy.wait()
    each(lambda t, dc: ask_copy(t, dc).wait_recv())
    to_scalar = pltpu.make_async_copy(table, table_s, table_sem)
    to_scalar.start()
    to_scalar.wait()

    def stage(t, dc):
        n = 2 * t + dc
        b = table_s[n, 0, 0] & (BLOCKS - 1)
        stage_a[n] = anc[b]
        stage_v[n] = sub[b]
        anchor_copy(t, dc).start()
        panel_copy(t, dc).start()

    each(stage)
    own = table_s[0, 0, 0] & (BLOCKS - 1)
    slots[0, 0:BA, :] = anc[own]
    panel[0] = sub[own]

    place = near & (BA - 1)
    flag = lax.shift_left(jnp.ones_like(owner), owner)
    lane = lax.broadcasted_iota(jnp.int32, (BA, BA), 1)
    for g in range(ROWS // BA):
        place_t = jnp.transpose(place[:, g * BA : (g + 1) * BA])
        flag_t = jnp.transpose(flag[:, g * BA : (g + 1) * BA])
        word = jnp.zeros((BA, BA), jnp.int32)
        for k in range(CAND):
            word = word | jnp.where(lane == place_t[:, k : k + 1], flag_t[:, k : k + 1], 0)
        words[g * BA : (g + 1) * BA, :] = word

    emb_copy.wait()

    @pl.loop(0, ROWS // BA)
    def _(g):
        rows = pl.ds(pl.multiple_of(g * BA, BA), BA)
        e = emb[rows, :].astype(jnp.float32)
        mean = jnp.sum(e * e, axis=1, keepdims=True) * (1.0 / D)
        rscale[rows, :] = jnp.broadcast_to(lax.rsqrt(mean + 1e-6) * SCALE, (BA, BA))

    sums[...] = jnp.zeros_like(sums)

    def pair(t):
        panel1[0:COLS, 0:BA] = panel[2 * t]
        panel1[0:COLS, BA:] = panel[2 * t + 1]
        anchors = slots[t]
        wide = anchors.astype(jnp.float32)
        mean = jnp.sum(wide * wide, axis=1, keepdims=True) * (1.0 / D)
        ascale = jnp.broadcast_to(lax.rsqrt(mean + 1e-6), (2 * BA, BA))
        ascale = jnp.transpose(ascale)[0:1, :]
        bit0 = bits_s[2 * t]
        bit1 = bits_s[2 * t + 1]

        @pl.loop(0, ROWS // RC)
        def _(g):
            rows = pl.ds(pl.multiple_of(g * RC, RC), RC)
            dots = nt(emb[rows, :], slots[t])
            word = words[rows, :]
            rs = rscale[rows, :]
            v1 = panel1[...]
            w0 = jnp.where((word & bit0) != 0, jnp.exp2(dots[:, :BA] * rs * ascale[:, :BA]), 0.0)
            w1 = jnp.where((word & bit1) != 0, jnp.exp2(dots[:, BA:] * rs * ascale[:, BA:]), 0.0)
            w = jnp.concatenate([w0, w1], axis=1)
            hi = w.astype(jnp.bfloat16)
            lo = (w - hi.astype(jnp.float32)).astype(jnp.bfloat16)
            high[t, rows, :] = hi
            low[t, rows, :] = lo
            sums[rows, :] += nt(hi, v1) + nt(lo, v1)

    zero = jnp.int32(0)
    anchor_copy(zero, 1).wait_recv()
    panel_copy(zero, 1).wait_recv()
    pair(zero)

    @pl.loop(1, 16)
    def _(t):
        for dc in range(2):
            anchor_copy(t, dc).wait_recv()
            panel_copy(t, dc).wait_recv()
        pair(t)

    @pl.loop(0, ROWS // BA)
    def _(g):
        rows = pl.ds(pl.multiple_of(g * BA, BA), BA)
        u = sums[rows, :]
        inverse = 1.0 / pltpu.roll(u, COLS, 1)
        proj = jnp.transpose(u * inverse * inverse)[0:COLS, :]
        hi = proj.astype(jnp.bfloat16)
        lhs[0:COLS, rows] = hi
        lhs[COLS:, rows] = (proj - hi.astype(jnp.float32)).astype(jnp.bfloat16)

    def product(t):
        r1 = nn(lhs[...], high[t])
        r2 = nn(lhs[0:COLS, :], low[t])
        return r1[0:COLS, :] + r1[COLS:, :] + r2

    @pl.loop(0, 15)
    def _(i):
        t = 15 - i
        g = product(t)
        for dc in range(2):
            give[2 * t + dc] = g[:, dc * BA : (dc + 1) * BA]
            return_copy(t, dc).start()

    g = product(zero)
    back[0] = g[:, 0:BA]
    give[1] = g[:, BA:]
    return_copy(zero, 1).start()

    acc[...] = jnp.zeros_like(acc)

    def collect(n):
        value = back[n]
        b = table_s[n, 0, 0] & (BLOCKS - 1)
        for i in range(BLOCKS):
            acc[i] += jnp.where(b == i, value, 0.0)

    @pl.loop(0, 15)
    def _(i):
        t = 15 - i
        for dc in range(2):
            return_copy(t, dc).wait_recv()
            collect(2 * t + dc)

    collect(0)
    return_copy(zero, 1).wait_recv()
    collect(1)

    def reduce_copy(k):
        to = lax.rem(z + k, PLANES)
        return pltpu.make_async_remote_copy(
            src_ref=acc.at[pl.ds(2 * to, 2)], dst_ref=part.at[k],
            send_sem=red_s.at[k], recv_sem=red_r.at[k],
            device_id=(to, y, a), device_id_type=MESH,
        )

    def gather_copy(k):
        to = lax.rem(z + k, PLANES)
        return pltpu.make_async_remote_copy(
            src_ref=whole.at[pl.ds(2 * z, 2)], dst_ref=whole.at[pl.ds(2 * z, 2)],
            send_sem=gat_s.at[k], recv_sem=gat_r.at[k],
            device_id=(to, y, a), device_id_type=MESH,
        )

    for k in (4, 3, 5, 2, 6, 1, 7):
        reduce_copy(k).start()
    total = acc[pl.ds(2 * z, 2)]
    for k in (1, 7, 2, 6, 3, 5, 4):
        reduce_copy(k).wait_recv()
        total = total + part[k]
    whole[pl.ds(2 * z, 2)] = total
    for k in (4, 3, 5, 2, 6, 1, 7):
        gather_copy(k).start()
    for k in range(1, PLANES):
        gather_copy(k).wait_recv()
    for b in range(BLOCKS):
        out_ref[:, b * BA : (b + 1) * BA] = whole[b]

    @pl.loop(1, PLANES)
    def _(k):
        reduce_copy(k).wait_send()
        gather_copy(k).wait_send()

    def drain(t, dc):
        ask_copy(t, dc).wait_send()
        anchor_copy(t, dc).wait_send()
        panel_copy(t, dc).wait_send()
        return_copy(t, dc).wait_send()

    each(drain)


def per_device(embeddings, anchors, subspace, nearest):
    dma = pltpu.SemaphoreType.DMA
    bf16, f32, i32 = jnp.bfloat16, jnp.float32, jnp.int32
    out = pl.pallas_call(
        kernel,
        out_shape=jax.ShapeDtypeStruct((COLS, BLOCKS * BA), f32),
        in_specs=[
            pl.BlockSpec(memory_space=pl.ANY),
            pl.BlockSpec(memory_space=pl.ANY),
            pl.BlockSpec(memory_space=pltpu.VMEM),
            pl.BlockSpec(memory_space=pltpu.VMEM),
        ],
        out_specs=pl.BlockSpec(memory_space=pltpu.VMEM),
        scratch_shapes=[
            pltpu.VMEM((ROWS, D), bf16),
            pltpu.VMEM((BLOCKS, BA, D), bf16),
            pltpu.VMEM((BLOCKS, COLS, BA), bf16),
            pltpu.VMEM((OWNERS, 128), i32),
            pltpu.VMEM((OWNERS, 1, 128), i32),
            pltpu.VMEM((OWNERS, 1, 128), i32),
            pltpu.SMEM((OWNERS, 1, 128), i32),
            pltpu.SMEM((OWNERS,), i32),
            pltpu.VMEM((OWNERS, BA, D), bf16),
            pltpu.VMEM((OWNERS, COLS, BA), bf16),
            pltpu.VMEM((16, 2 * BA, D), bf16),
            pltpu.VMEM((OWNERS, COLS, BA), bf16),
            pltpu.VMEM((BA, 2 * BA), bf16),
            pltpu.VMEM((ROWS, BA), i32),
            pltpu.VMEM((ROWS, BA), f32),
            pltpu.VMEM((16, ROWS, 2 * BA), bf16),
            pltpu.VMEM((16, ROWS, 2 * BA), bf16),
            pltpu.VMEM((ROWS, BA), f32),
            pltpu.VMEM((BA, ROWS), bf16),
            pltpu.VMEM((OWNERS, COLS, BA), f32),
            pltpu.VMEM((OWNERS, COLS, BA), f32),
            pltpu.VMEM((BLOCKS, COLS, BA), f32),
            pltpu.VMEM((PLANES, 2, COLS, BA), f32),
            pltpu.VMEM((BLOCKS, COLS, BA), f32),
            dma((2,)),
            dma,
        ]
        + [dma((OWNERS,))] * 8
        + [dma((PLANES,))] * 4,
        compiler_params=pltpu.CompilerParams(
            collective_id=0, has_side_effects=True, vmem_limit_bytes=62 * 1024 * 1024
        ),
    )(embeddings, anchors.reshape(BLOCKS, BA, D), subspace.T, nearest.T)
    return out.T


def solution(mesh):
    in_specs = (
        P(("samp", "arow", "acol"), None),
        P(("arow", "acol"), None),
        P(("arow", "acol"), None),
        P(("samp", "arow", "acol"), None),
    )
    return jax.shard_map(
        per_device, mesh=mesh, in_specs=in_specs, out_specs=P(("arow", "acol"), None),
        check_vma=False,
    )
```

time: 471 us -> 151 us (0.32)
  matrix products: 153 us -> 0 us
  Pallas kernels: 0 us -> 148 us
  waiting for transfers between devices: 143 us -> 0 us
  other arithmetic: 68.2 us -> 0 us
  local copies, waits for them, and re-layouts: 56.2 us -> 1.87 us
  blocking collectives: 20.2 us -> 0 us
  between operations: 13.5 us -> 0.01 us
  starting transfers between devices: 12.3 us -> 0 us
    dot_general x19 -> x0, matrix products: 153 us -> none  [the longest x6 85.2 us: one_block(): lax.dot_general(group_rows, flat_anchor, (((1,), (1,)), ((), ())), prefer...]
    pallas_call x0 -> x1, Pallas kernels: none -> 148 us  [per_device(): pl.pallas_call(kernel, out_shape=jax.ShapeDtypeStruct((COLS, BLOCKS * BA)...]
    all_to_all x2 -> x0, waiting for transfers between devices: 90.6 us -> none  [the longest x1 84.3 us: sent_together(): lax.all_to_all(both, axis, split_axis=split_dim, concat_axis=concat_dim,...]
    all_gather x1 -> x0, waiting for transfers between devices: 52 us -> none  [total_of_pieces(): return lax.all_gather(value, axis).sum(0)]
    dot_general x6 -> x0, other arithmetic: 43.9 us -> none  [one_block(): jnp.dot(zmatrix, flat_panel, precision=lax.Precision.HIGHEST, preferred_e...]
    all_to_all x1 -> x0, blocking collectives: 20.2 us -> none  [per_device(): lax.all_to_all(outgoing.reshape(owners, BA, COLS), ('arow', 'acol'), spli...]
    reduce_sum x14 -> x0, other arithmetic: 14.4 us -> none  [the longest x6 6.91 us: one_block(): row_scale = lax.rsqrt(jnp.mean(rows_float * rows_float, axis=1) + 1e-06)]
    all_to_all x2 -> x0, starting transfers between devices: 12.2 us -> none  [the longest x1 7.32 us: from_everyone(): lax.all_to_all(jnp.broadcast_to(value[None], (devices, *value.shape)), ax...]
  transfers between devices with their start and end apart: 3 -> 0, of which waited for: 3 -> 0; matrix products, arithmetic and copies ran while one was open for 0% -> 0% of each run, Pallas kernels for 0% -> 0%
where the time goes in v1:
time: 151 us; the launch traced here: 150 us
  Pallas kernels  148 us (98%)
  local copies, waits for them, and re-layouts  1.87 us (1%)
    pallas_call x1, Pallas kernels, per_device(): pl.pallas_call(kernel, out_shape=jax.ShapeDtypeStruct((COLS, BLOCKS * BA)...  148 us

profile of v1, /device:TPU:32, one launch (start us, length us, event | category | flops | bytes accessed | tf_op | source)
XLA Modules:
  0.0 149.6 jit_solution(16156526511010925161)
XLA Ops:
  0.0 147.8 %shard_map.46 = f32[64,2048]{1,0:T(8,128)} custom-call(bf16[1536,768]{1,0:T(8,128)(2,1)} %emb_hbm.1, bf16[16,128,768]{2,1,0:T(8,128)(2,1)} %bitcast.4, bf16[64,2048]{1,0:T(8,128)(2,1)} %bitcast.6, s32[8,1536]{1,0:T(8,128)} %bitcast.7), custom_call_target="tpu_custom_call" | custom-call | tf_op jit(solution)/shard_map/pallas_call | solution.py:341
  147.8 1.9 %copy.6 = f32[2048,64]{0,1:T(8,128)} copy(f32[2048,64]{0,1:T(8,128)} %bitcast.5) | data formatting | bytes 1048576

commit v2 on v1

--- a/solution.py
+++ b/solution.py
@@ -15,7 +15,8 @@
 BLOCKS = 16
 ROWS = 1536
 PLANES = 8
-RC = 256
+RC = 768
+HOPS = 4
 MESH = pl.DeviceIdType.MESH
 SCALE = 20.0 * 1.4426950408889634 / D
 
@@ -46,8 +47,8 @@
 
 
 def kernel(
-    emb_hbm, anc_hbm, sub_ref, near_ref, out_ref,
-    emb, anc, sub, best, ask, table, table_s, bits_s,
+    emb_hbm, anc_hbm, sub_hbm, near_hbm, out_ref,
+    near_v, sub_v, emb, anc, sub, best, ask, table, table_s, bits_s,
     stage_a, stage_v, slots, panel, panel1, words, rscale, high, low, sums, lhs,
     give, back, acc, part, whole,
     local_sem, table_sem, ask_s, ask_r, anc_s, anc_r, pan_s, pan_r, ret_s, ret_r,
@@ -75,7 +76,11 @@
 
     emb_copy = pltpu.make_async_copy(emb_hbm, emb, local_sem.at[0])
     anc_copy = pltpu.make_async_copy(anc_hbm, anc, local_sem.at[1])
+    near_copy = pltpu.make_async_copy(near_hbm, near_v, local_sem.at[2])
+    sub_copy = pltpu.make_async_copy(sub_hbm, sub_v, local_sem.at[3])
+    near_copy.start()
     anc_copy.start()
+    sub_copy.start()
     emb_copy.start()
 
     barrier = pltpu.get_barrier_semaphore()
@@ -93,7 +98,8 @@
             barrier, inc=1, device_id=(lax.rem(z + i, PLANES), y, a), device_id_type=MESH
         )
 
-    near = near_ref[...]
+    near_copy.wait()
+    near = near_v[...]
     owner = near >> 11
     block = (near >> 7) & 15
     for o in range(OWNERS):
@@ -153,8 +159,9 @@
 
     each(lambda t, dc: ask_copy(t, dc).start())
 
+    sub_copy.wait()
     for b in range(BLOCKS):
-        sub[b] = sub_ref[:, b * BA : (b + 1) * BA]
+        sub[b] = sub_v[:, b * BA : (b + 1) * BA]
     panel1[COLS:, :] = jnp.ones((BA - COLS, 2 * BA), jnp.bfloat16)
     table[0] = ask[me]
 
@@ -244,9 +251,8 @@
             panel_copy(t, dc).wait_recv()
         pair(t)
 
-    @pl.loop(0, ROWS // BA)
-    def _(g):
-        rows = pl.ds(pl.multiple_of(g * BA, BA), BA)
+    for g in range(ROWS // BA):
+        rows = pl.ds(g * BA, BA)
         u = sums[rows, :]
         inverse = 1.0 / pltpu.roll(u, COLS, 1)
         proj = jnp.transpose(u * inverse * inverse)[0:COLS, :]
@@ -291,40 +297,68 @@
     return_copy(zero, 1).wait_recv()
     collect(1)
 
-    def reduce_copy(k):
-        to = lax.rem(z + k, PLANES)
-        return pltpu.make_async_remote_copy(
-            src_ref=acc.at[pl.ds(2 * to, 2)], dst_ref=part.at[k],
-            send_sem=red_s.at[k], recv_sem=red_r.at[k],
+    half = COLS // 2
+    streams = [(p, way) for p in range(4) for way in range(2)]
+
+    def hops(p, way):
+        return HOPS if p // 2 == way else HOPS - 1
+
+    def slab(way, distance):
+        return lax.rem(z + (PLANES + distance if way == 0 else PLANES - distance), PLANES)
+
+    def reduce_copy(p, way, s):
+        to = slab(way, 1)
+        of = slab(way, HOPS + 1 - s)
+        return pltpu.make_async_remote_copy(
+            src_ref=acc.at[2 * of + p // 2, pl.ds(p % 2 * half, half)], dst_ref=part.at[way, p, s - 1],
+            send_sem=red_s.at[way, p, s - 1], recv_sem=red_r.at[way, p, s - 1],
             device_id=(to, y, a), device_id_type=MESH,
         )
 
-    def gather_copy(k):
-        to = lax.rem(z + k, PLANES)
-        return pltpu.make_async_remote_copy(
-            src_ref=whole.at[pl.ds(2 * z, 2)], dst_ref=whole.at[pl.ds(2 * z, 2)],
-            send_sem=gat_s.at[k], recv_sem=gat_r.at[k],
+    def gather_copy(p, way, s):
+        to = slab(way, 1)
+        where = whole.at[slab(1 - way, s - 1), p]
+        return pltpu.make_async_remote_copy(
+            src_ref=where, dst_ref=where,
+            send_sem=gat_s.at[way, p, s - 1], recv_sem=gat_r.at[way, p, s - 1],
             device_id=(to, y, a), device_id_type=MESH,
         )
 
-    for k in (4, 3, 5, 2, 6, 1, 7):
-        reduce_copy(k).start()
-    total = acc[pl.ds(2 * z, 2)]
-    for k in (1, 7, 2, 6, 3, 5, 4):
-        reduce_copy(k).wait_recv()
-        total = total + part[k]
-    whole[pl.ds(2 * z, 2)] = total
-    for k in (4, 3, 5, 2, 6, 1, 7):
-        gather_copy(k).start()
-    for k in range(1, PLANES):
-        gather_copy(k).wait_recv()
+    for s in range(1, HOPS + 1):
+        for p in range(4):
+            ready = []
+            for way in range(2):
+                first = HOPS + 1 - hops(p, way)
+                if s < first:
+                    continue
+                if s > first:
+                    reduce_copy(p, way, s - 1).wait_recv()
+                    of = slab(way, HOPS + 1 - s)
+                    acc[2 * of + p // 2, p % 2 * half : (p % 2 + 1) * half] += part[way, p, s - 2]
+                ready.append(reduce_copy(p, way, s))
+            for copy in ready:
+                copy.start()
+    for p in range(4):
+        for way in range(2):
+            reduce_copy(p, way, HOPS).wait_recv()
+        total = acc[2 * z + p // 2, p % 2 * half : (p % 2 + 1) * half]
+        whole[z, p] = total + part[0, p, HOPS - 1] + part[1, p, HOPS - 1]
+        for way in range(2):
+            gather_copy(p, way, 1).start()
+    for s in range(2, HOPS + 1):
+        for p, way in streams:
+            if s <= hops(p, way):
+                gather_copy(p, way, s - 1).wait_recv()
+                gather_copy(p, way, s).start()
+    for p, way in streams:
+        gather_copy(p, way, hops(p, way)).wait_recv()
     for b in range(BLOCKS):
-        out_ref[:, b * BA : (b + 1) * BA] = whole[b]
-
-    @pl.loop(1, PLANES)
-    def _(k):
-        reduce_copy(k).wait_send()
-        gather_copy(k).wait_send()
+        for h in range(2):
+            out_ref[h * half : (h + 1) * half, b * BA : (b + 1) * BA] = whole[b // 2, b % 2 * 2 + h]
+    for p, way in streams:
+        for s in range(1, hops(p, way) + 1):
+            reduce_copy(p, way, HOPS + 1 - s).wait_send()
+            gather_copy(p, way, s).wait_send()
 
     def drain(t, dc):
         ask_copy(t, dc).wait_send()
@@ -344,11 +378,13 @@
         in_specs=[
             pl.BlockSpec(memory_space=pl.ANY),
             pl.BlockSpec(memory_space=pl.ANY),
-            pl.BlockSpec(memory_space=pltpu.VMEM),
-            pl.BlockSpec(memory_space=pltpu.VMEM),
+            pl.BlockSpec(memory_space=pl.ANY),
+            pl.BlockSpec(memory_space=pl.ANY),
         ],
         out_specs=pl.BlockSpec(memory_space=pltpu.VMEM),
         scratch_shapes=[
+            pltpu.VMEM((CAND, ROWS), i32),
+            pltpu.VMEM((COLS, BLOCKS * BA), bf16),
             pltpu.VMEM((ROWS, D), bf16),
             pltpu.VMEM((BLOCKS, BA, D), bf16),
             pltpu.VMEM((BLOCKS, COLS, BA), bf16),
@@ -371,15 +407,15 @@
             pltpu.VMEM((OWNERS, COLS, BA), f32),
             pltpu.VMEM((OWNERS, COLS, BA), f32),
             pltpu.VMEM((BLOCKS, COLS, BA), f32),
-            pltpu.VMEM((PLANES, 2, COLS, BA), f32),
-            pltpu.VMEM((BLOCKS, COLS, BA), f32),
-            dma((2,)),
+            pltpu.VMEM((2, 4, HOPS, COLS // 2, BA), f32),
+            pltpu.VMEM((PLANES, 4, COLS // 2, BA), f32),
+            dma((4,)),
             dma,
         ]
         + [dma((OWNERS,))] * 8
-        + [dma((PLANES,))] * 4,
+        + [dma((2, 4, HOPS))] * 4,
         compiler_params=pltpu.CompilerParams(
-            collective_id=0, has_side_effects=True, vmem_limit_bytes=62 * 1024 * 1024
+            collective_id=0, has_side_effects=True, vmem_limit_bytes=67_043_328
         ),
     )(embeddings, anchors.reshape(BLOCKS, BA, D), subspace.T, nearest.T)
     return out.T

time: 151 us -> 146 us (0.967)
  Pallas kernels: 148 us -> 144 us
    pallas_call x1, Pallas kernels: 148 us -> 144 us  [per_device(): pl.pallas_call(kernel, out_shape=jax.ShapeDtypeStruct((COLS, BLOCKS * BA)...]
where the time goes in v2:
time: 146 us
  Pallas kernels  144 us (99%)
  local copies, waits for them, and re-layouts  1.87 us (1%)
    pallas_call x1, Pallas kernels, per_device(): pl.pallas_call(kernel, out_shape=jax.ShapeDtypeStruct((COLS, BLOCKS * BA)...  144 us

profile of v2, /device:TPU:32, one launch (start us, length us, event | category | flops | bytes accessed | tf_op | source)
XLA Modules:
  0.0 146.1 jit_solution(9060943921638699561)
XLA Ops:
  0.0 144.2 %shard_map.46 = f32[64,2048]{1,0:T(8,128)} custom-call(bf16[1536,768]{1,0:T(8,128)(2,1)} %emb_hbm.1, bf16[16,128,768]{2,1,0:T(8,128)(2,1)} %bitcast.4, bf16[64,2048]{1,0:T(8,128)(2,1)} %bitcast.6, s32[8,1536]{1,0:T(8,128)} %bitcast.7), custom_call_target="tpu_custom_call" | custom-call | tf_op jit(solution)/shard_map/pallas_call | solution.py:375
  144.2 1.9 %copy.6 = f32[2048,64]{0,1:T(8,128)} copy(f32[2048,64]{0,1:T(8,128)} %bitcast.5) | data formatting | bytes 1048576

commit v3 on v2

--- a/solution.py
+++ b/solution.py
@@ -16,7 +16,6 @@
 ROWS = 1536
 PLANES = 8
 RC = 768
-HOPS = 4
 MESH = pl.DeviceIdType.MESH
 SCALE = 20.0 * 1.4426950408889634 / D
 
@@ -47,12 +46,12 @@
 
 
 def kernel(
-    emb_hbm, anc_hbm, sub_hbm, near_hbm, out_ref,
+    emb_hbm, anc_hbm, sub_hbm, near_hbm, out_hbm,
     near_v, sub_v, emb, anc, sub, best, ask, table, table_s, bits_s,
     stage_a, stage_v, slots, panel, panel1, words, rscale, high, low, sums, lhs,
     give, back, acc, part, whole,
     local_sem, table_sem, ask_s, ask_r, anc_s, anc_r, pan_s, pan_r, ret_s, ret_r,
-    red_s, red_r, gat_s, gat_r,
+    red_s, red_r, gat_s, gat_r, out_sem,
 ):
     z = lax.axis_index("samp")
     y = lax.axis_index("arow")
@@ -300,65 +299,96 @@
     half = COLS // 2
     streams = [(p, way) for p in range(4) for way in range(2)]
 
-    def hops(p, way):
-        return HOPS if p // 2 == way else HOPS - 1
-
     def slab(way, distance):
         return lax.rem(z + (PLANES + distance if way == 0 else PLANES - distance), PLANES)
 
-    def reduce_copy(p, way, s):
-        to = slab(way, 1)
-        of = slab(way, HOPS + 1 - s)
-        return pltpu.make_async_remote_copy(
-            src_ref=acc.at[2 * of + p // 2, pl.ds(p % 2 * half, half)], dst_ref=part.at[way, p, s - 1],
-            send_sem=red_s.at[way, p, s - 1], recv_sem=red_r.at[way, p, s - 1],
-            device_id=(to, y, a), device_id_type=MESH,
-        )
-
-    def gather_copy(p, way, s):
-        to = slab(way, 1)
-        where = whole.at[slab(1 - way, s - 1), p]
+    reduce_hops = ((2, 4), (1, 3), (2, 2), (1, 1))
+
+    def reduce_copy(p, way, slot):
+        step, of = reduce_hops[slot]
+        return pltpu.make_async_remote_copy(
+            src_ref=acc.at[2 * slab(way, of) + p // 2, pl.ds(p % 2 * half, half)],
+            dst_ref=part.at[way, p, slot],
+            send_sem=red_s.at[way, p, slot], recv_sem=red_r.at[way, p, slot],
+            device_id=(slab(way, step), y, a), device_id_type=MESH,
+        )
+
+    gather_hops = ((1, 0), (2, 0), (1, 2), (2, 2))
+
+    def gather_copy(p, way, slot):
+        step, back_to = gather_hops[slot]
+        where = whole.at[slab(1 - way, back_to), p]
         return pltpu.make_async_remote_copy(
             src_ref=where, dst_ref=where,
-            send_sem=gat_s.at[way, p, s - 1], recv_sem=gat_r.at[way, p, s - 1],
-            device_id=(to, y, a), device_id_type=MESH,
-        )
-
-    for s in range(1, HOPS + 1):
-        for p in range(4):
-            ready = []
-            for way in range(2):
-                first = HOPS + 1 - hops(p, way)
-                if s < first:
-                    continue
-                if s > first:
-                    reduce_copy(p, way, s - 1).wait_recv()
-                    of = slab(way, HOPS + 1 - s)
-                    acc[2 * of + p // 2, p % 2 * half : (p % 2 + 1) * half] += part[way, p, s - 2]
-                ready.append(reduce_copy(p, way, s))
-            for copy in ready:
-                copy.start()
+            send_sem=gat_s.at[way, p, slot], recv_sem=gat_r.at[way, p, slot],
+            device_id=(slab(way, step), y, a), device_id_type=MESH,
+        )
+
+    def result_copy(p, origin):
+        lanes = pl.ds(pl.multiple_of((2 * origin + p // 2) * BA, BA), BA)
+        return pltpu.make_async_copy(
+            whole.at[origin, p], out_hbm.at[pl.ds(p % 2 * half, half), lanes], out_sem.at[origin, p]
+        )
+
+    def far(p, way):
+        return p // 2 == way
+
+    for p, way in streams:
+        if far(p, way):
+            reduce_copy(p, way, 0).start()
+    for p, way in streams:
+        reduce_copy(p, way, 1).start()
+    for p, way in streams:
+        reduce_copy(p, way, 3).start()
     for p in range(4):
-        for way in range(2):
-            reduce_copy(p, way, HOPS).wait_recv()
+        columns = slice(p % 2 * half, (p % 2 + 1) * half)
+        for way in range(2):
+            reduce_copy(p, way, 1).wait_recv()
+            value = part[way, p, 1]
+            if far(p, way):
+                reduce_copy(p, way, 0).wait_recv()
+                value = value + part[way, p, 0]
+            acc[2 * slab(way, 2) + p // 2, columns] += value
+        for way in range(2):
+            reduce_copy(p, way, 2).start()
+    for p in range(4):
         total = acc[2 * z + p // 2, p % 2 * half : (p % 2 + 1) * half]
-        whole[z, p] = total + part[0, p, HOPS - 1] + part[1, p, HOPS - 1]
+        for way in range(2):
+            reduce_copy(p, way, 3).wait_recv()
+            total = total + part[way, p, 3]
+        for way in range(2):
+            reduce_copy(p, way, 2).wait_recv()
+            total = total + part[way, p, 2]
+        whole[z, p] = total
         for way in range(2):
             gather_copy(p, way, 1).start()
-    for s in range(2, HOPS + 1):
-        for p, way in streams:
-            if s <= hops(p, way):
-                gather_copy(p, way, s - 1).wait_recv()
-                gather_copy(p, way, s).start()
-    for p, way in streams:
-        gather_copy(p, way, hops(p, way)).wait_recv()
-    for b in range(BLOCKS):
-        for h in range(2):
-            out_ref[h * half : (h + 1) * half, b * BA : (b + 1) * BA] = whole[b // 2, b % 2 * 2 + h]
-    for p, way in streams:
-        for s in range(1, hops(p, way) + 1):
-            reduce_copy(p, way, HOPS + 1 - s).wait_send()
-            gather_copy(p, way, s).wait_send()
+        for way in range(2):
+            gather_copy(p, way, 0).start()
+        result_copy(p, z).start()
+    for p, way in streams:
+        gather_copy(p, way, 1).wait_recv()
+        if far(p, way):
+            gather_copy(p, way, 3).start()
+        gather_copy(p, way, 2).start()
+        result_copy(p, slab(1 - way, 2)).start()
+    for p, way in streams:
+        gather_copy(p, way, 0).wait_recv()
+        result_copy(p, slab(1 - way, 1)).start()
+    for p, way in streams:
+        gather_copy(p, way, 2).wait_recv()
+        result_copy(p, slab(1 - way, 3)).start()
+        if far(p, way):
+            gather_copy(p, way, 3).wait_recv()
+            result_copy(p, slab(1 - way, 4)).start()
+    for p, way in streams:
+        for slot in range(4):
+            if slot > 0 or far(p, way):
+                reduce_copy(p, way, slot).wait_send()
+            if slot < 3 or far(p, way):
+                gather_copy(p, way, slot).wait_send()
+    for p in range(4):
+        for origin in range(PLANES):
+            result_copy(p, origin).wait()
 
     def drain(t, dc):
         ask_copy(t, dc).wait_send()
@@ -381,7 +411,7 @@
             pl.BlockSpec(memory_space=pl.ANY),
             pl.BlockSpec(memory_space=pl.ANY),
         ],
-        out_specs=pl.BlockSpec(memory_space=pltpu.VMEM),
+        out_specs=pl.BlockSpec(memory_space=pl.ANY),
         scratch_shapes=[
             pltpu.VMEM((CAND, ROWS), i32),
             pltpu.VMEM((COLS, BLOCKS * BA), bf16),
@@ -407,13 +437,14 @@
             pltpu.VMEM((OWNERS, COLS, BA), f32),
             pltpu.VMEM((OWNERS, COLS, BA), f32),
             pltpu.VMEM((BLOCKS, COLS, BA), f32),
-            pltpu.VMEM((2, 4, HOPS, COLS // 2, BA), f32),
+            pltpu.VMEM((2, 4, 4, COLS // 2, BA), f32),
             pltpu.VMEM((PLANES, 4, COLS // 2, BA), f32),
             dma((4,)),
             dma,
         ]
         + [dma((OWNERS,))] * 8
-        + [dma((2, 4, HOPS))] * 4,
+        + [dma((2, 4, 4))] * 4
+        + [dma((PLANES, 4))],
         compiler_params=pltpu.CompilerParams(
             collective_id=0, has_side_effects=True, vmem_limit_bytes=67_043_328
         ),

time: 146 us -> 138 us (0.945)
  Pallas kernels: 144 us -> 136 us
    pallas_call x1, Pallas kernels: 144 us -> 136 us  [per_device(): pl.pallas_call(kernel, out_shape=jax.ShapeDtypeStruct((COLS, BLOCKS * BA)...]
where the time goes in v3:
time: 138 us
  Pallas kernels  136 us (99%)
  local copies, waits for them, and re-layouts  1.87 us (1%)
    pallas_call x1, Pallas kernels, per_device(): pl.pallas_call(kernel, out_shape=jax.ShapeDtypeStruct((COLS, BLOCKS * BA)...  136 us

profile of v3, /device:TPU:32, one launch (start us, length us, event | category | flops | bytes accessed | tf_op | source)
XLA Modules:
  0.0 138.0 jit_solution(2665890150513504613)
XLA Ops:
  0.0 136.1 %shard_map.46 = f32[64,2048]{1,0:T(8,128)} custom-call(bf16[1536,768]{1,0:T(8,128)(2,1)} %emb_hbm.1, bf16[16,128,768]{2,1,0:T(8,128)(2,1)} %bitcast.4, bf16[64,2048]{1,0:T(8,128)(2,1)} %bitcast.6, s32[8,1536]{1,0:T(8,128)} %bitcast.7), custom_call_target="tpu_custom_call" | custom-call | tf_op jit(solution)/shard_map/pallas_call | solution.py:405
  136.1 1.9 %copy.6 = f32[2048,64]{0,1:T(8,128)} copy(f32[2048,64]{0,1:T(8,128)} %bitcast.5) | data formatting | bytes 1048576

commit v4 on v3

--- a/solution.py
+++ b/solution.py
@@ -171,10 +171,20 @@
             bits_s[2 * t + dc] = lax.shift_left(jnp.int32(1), h[1] * 8 + h[2])
 
     anc_copy.wait()
-    each(lambda t, dc: ask_copy(t, dc).wait_recv())
-    to_scalar = pltpu.make_async_copy(table, table_s, table_sem)
-    to_scalar.start()
-    to_scalar.wait()
+
+    def to_scalar(i):
+        part_of = pl.ds(16 * i, 16)
+        return pltpu.make_async_copy(table.at[part_of], table_s.at[part_of], table_sem.at[i])
+
+    ask_copy(jnp.int32(0), 1).wait_recv()
+    for i in range(2):
+
+        @pl.loop(max(1, 8 * i), 8 * i + 8)
+        def _(t):
+            for dc in range(2):
+                ask_copy(t, dc).wait_recv()
+
+        to_scalar(i).start()
 
     def stage(t, dc):
         n = 2 * t + dc
@@ -184,7 +194,18 @@
         anchor_copy(t, dc).start()
         panel_copy(t, dc).start()
 
-    each(stage)
+    to_scalar(0).wait()
+    stage(jnp.int32(0), 1)
+    for i in range(2):
+
+        @pl.loop(max(1, 8 * i), 8 * i + 8)
+        def _(t):
+            stage(t, 0)
+            stage(t, 1)
+
+        if i == 0:
+            to_scalar(1).wait()
+
     own = table_s[0, 0, 0] & (BLOCKS - 1)
     slots[0, 0:BA, :] = anc[own]
     panel[0] = sub[own]
@@ -210,6 +231,7 @@
         rscale[rows, :] = jnp.broadcast_to(lax.rsqrt(mean + 1e-6) * SCALE, (BA, BA))
 
     sums[...] = jnp.zeros_like(sums)
+    acc[...] = jnp.zeros_like(acc)
 
     def pair(t):
         panel1[0:COLS, 0:BA] = panel[2 * t]
@@ -277,7 +299,12 @@
     give[1] = g[:, BA:]
     return_copy(zero, 1).start()
 
-    acc[...] = jnp.zeros_like(acc)
+    def drain(t, dc):
+        ask_copy(t, dc).wait_send()
+        anchor_copy(t, dc).wait_send()
+        panel_copy(t, dc).wait_send()
+
+    each(drain)
 
     def collect(n):
         value = back[n]
@@ -390,13 +417,7 @@
         for origin in range(PLANES):
             result_copy(p, origin).wait()
 
-    def drain(t, dc):
-        ask_copy(t, dc).wait_send()
-        anchor_copy(t, dc).wait_send()
-        panel_copy(t, dc).wait_send()
-        return_copy(t, dc).wait_send()
-
-    each(drain)
+    each(lambda t, dc: return_copy(t, dc).wait_send())
 
 
 def per_device(embeddings, anchors, subspace, nearest):
@@ -440,7 +461,7 @@
             pltpu.VMEM((2, 4, 4, COLS // 2, BA), f32),
             pltpu.VMEM((PLANES, 4, COLS // 2, BA), f32),
             dma((4,)),
-            dma,
+            dma((2,)),
         ]
         + [dma((OWNERS,))] * 8
         + [dma((2, 4, 4))] * 4

time: 138 us -> 138 us (level)
  no operation moved by 1% of the time
where the time goes in v4:
time: 138 us; the launch traced here: 137 us
  Pallas kernels  135 us (98%)
  local copies, waits for them, and re-layouts  1.87 us (1%)
    pallas_call x1, Pallas kernels, per_device(): pl.pallas_call(kernel, out_shape=jax.ShapeDtypeStruct((COLS, BLOCKS * BA)...  135 us

profile of v4, /device:TPU:32, one launch (start us, length us, event | category | flops | bytes accessed | tf_op | source)
XLA Modules:
  0.0 137.3 jit_solution(10653047840985769402)
XLA Ops:
  0.0 135.4 %shard_map.46 = f32[64,2048]{1,0:T(8,128)} custom-call(bf16[1536,768]{1,0:T(8,128)(2,1)} %emb_hbm.1, bf16[16,128,768]{2,1,0:T(8,128)(2,1)} %bitcast.4, bf16[64,2048]{1,0:T(8,128)(2,1)} %bitcast.6, s32[8,1536]{1,0:T(8,128)} %bitcast.7), custom_call_target="tpu_custom_call" | custom-call | tf_op jit(solution)/shard_map/pallas_call | solution.py:426
  135.4 1.9 %copy.6 = f32[2048,64]{0,1:T(8,128)} copy(f32[2048,64]{0,1:T(8,128)} %bitcast.5) | data formatting | bytes 1048576
